TPU v7x, 128 devices: a whole 4x4x4 slice. The times are simulated.
128 devices in a mesh: req: 32 (over z, y, x_hi), tensor: 4 (over x_lo, core).
Axes of the slice: x: 4 (x_hi: 2, x_lo: 2; x = x_hi * 2 + x_lo), y: 4, z: 4, core: 2. Of those that a mesh axis runs over, the one named last changes fastest.
Arguments:
- span_in: bfloat16 [64, 512, 2048], P('req'), may hold values from -6 to 6
- w_qkv: bfloat16 [3, 2048, 2048], P(None, None, 'tensor'), may hold values from -1 to 1
- qk_gain: bfloat16 [2, 2048], P(None, 'tensor'), may hold values from 0.099609375 to 1.8984375
- w_out: bfloat16 [2048, 2048], P('tensor'), may hold values from -1 to 1
- post_gain: bfloat16 [2048], P('tensor'), may hold values from 0.099609375 to 1.8984375
- kv_pool: bfloat16 [4, 2048, 16, 2048], P(None, 'req', None, 'tensor'), may hold values from -66 to 66
- block_table: int32 [64, 32], replicated, may hold values from 0 to 63, as said below
- request_order: int32 [64], replicated, may hold values from 0 to 63, each once
- lengths: int32 [64], replicated, may hold values from 1 to 512, as said below
Outputs:
- span_out: bfloat16 [64, 512, 2048], P('req', None, 'tensor')
- relaid_cache: bfloat16 [4, 64, 512, 2048], P(None, 'req', None, 'tensor')
Inputs may be any that keep to these rules, and one draw needn't show every extreme that they name: `block_table`: entry (r, j) is the slot, among the 64 slots of the req index j modulo the number of req devices, that holds block j of request r; each slot of each req index is named once. `lengths`: some request has exactly 512 cached tokens.
All inputs are finite; a program needn't handle non-finite values.
Results may differ from a plain program's by a relative error of at most 0.0095.
Values may be sent and summed in bfloat16 or wider, within the bound.
A program may use at most 192 MiB of HBM per device.

v0:
```python
import jax
import jax.numpy as jnp
from jax import lax
from jax.sharding import PartitionSpec as P

HD = 128


norm_eps = 1e-06
rope_base = 500000.0


def rotate(values, positions):
    half_dim = values.shape[-1] // 2
    frequency = rope_base ** (-jnp.arange(half_dim, dtype=jnp.float32) * (2.0 / values.shape[-1]))
    angles = positions[:, None] * frequency[None, :]
    cosine = jnp.cos(angles)[:, None, :]
    sine_part = jnp.sin(angles)[:, None, :]
    first_half = values[..., :half_dim]
    second_half = values[..., half_dim:]
    return jnp.concatenate(
        [
            first_half * cosine - second_half * sine_part,
            second_half * cosine + first_half * sine_part,
        ],
        axis=-1,
    )


def on_device(
    span_in, w_qkv, qk_gain, w_out, post_gain, kv_pool, block_table, request_order, lengths
):
    req_count = lax.axis_size("req")
    req_index = lax.axis_index("req")
    per_device = span_in.shape[0]
    span_len = span_in.shape[1]
    full_width = span_in.shape[2]
    part_width = w_qkv.shape[2]
    block_len = kv_pool.shape[2]
    blocks_each = block_table.shape[1] // req_count
    wanted = jnp.transpose(request_order.reshape(req_count, per_device))
    table_rows = jnp.take(block_table, wanted, axis=0)
    local_blocks = req_index + req_count * jnp.arange(blocks_each, dtype=jnp.int32)
    picked = jnp.take(table_rows, local_blocks, axis=2)
    picked = jnp.transpose(picked, (0, 2, 1)).reshape(-1)
    gathered = jnp.take(kv_pool, picked, axis=1)
    received = lax.all_to_all(
        gathered.reshape(
            kv_pool.shape[0], per_device, blocks_each, req_count * block_len, part_width
        ),
        "req",
        split_axis=3,
        concat_axis=3,
        tiled=True,
    )
    relaid = received.reshape(kv_pool.shape[0], per_device, -1, part_width)
    my_order = lax.dynamic_slice_in_dim(request_order, req_index * per_device, per_device)
    my_lengths = jnp.take(lengths, my_order)
    flat_in = span_in.reshape(-1, full_width)
    projected = jnp.einsum("rd,mdw->mrw", flat_in, w_qkv, preferred_element_type=jnp.float32)
    queries = projected[0]
    keys_new = projected[1]
    values_new = projected[2].astype(jnp.bfloat16)
    query_sq, key_sq = lax.psum(
        (jnp.sum(queries * queries, axis=-1), jnp.sum(keys_new * keys_new, axis=-1)), "tensor"
    )
    norm_gains = qk_gain.astype(jnp.float32)
    queries = queries * lax.rsqrt(query_sq / full_width + norm_eps)[:, None] * norm_gains[0]
    keys_new = keys_new * lax.rsqrt(key_sq / full_width + norm_eps)[:, None] * norm_gains[1]
    positions = (
        my_lengths.astype(jnp.float32)[:, None] + jnp.arange(span_len, dtype=jnp.float32)[None, :]
    ).reshape(-1)
    local_heads = part_width // HD
    query_rot = rotate(queries.reshape(-1, local_heads, HD), positions).astype(jnp.bfloat16)
    query_rot = query_rot.reshape(per_device, span_len, local_heads, HD)
    key_rot = rotate(keys_new.reshape(-1, local_heads, HD), positions).astype(jnp.bfloat16)
    key_rot = key_rot.reshape(per_device, span_len, local_heads, HD)
    context = relaid.shape[2]
    all_keys = jnp.concatenate(
        [relaid[0].reshape(per_device, context, local_heads, HD), key_rot], axis=1
    )
    all_values = jnp.concatenate(
        [
            relaid[1].reshape(per_device, context, local_heads, HD),
            values_new.reshape(per_device, span_len, local_heads, HD),
        ],
        axis=1,
    )
    scores = jnp.einsum(
        "bqhd,bkhd->bhqk", query_rot, all_keys, preferred_element_type=jnp.float32
    ) * HD ** (-0.5)
    cache_live = jnp.arange(context, dtype=jnp.int32)[None, :] < my_lengths[:, None]
    causal = jnp.arange(span_len)[None, :] <= jnp.arange(span_len)[:, None]
    live_mask = jnp.concatenate(
        [
            jnp.broadcast_to(cache_live[:, None, :], (per_device, span_len, context)),
            jnp.broadcast_to(causal[None], (per_device, span_len, span_len)),
        ],
        axis=2,
    )
    scores = jnp.where(live_mask[:, None], scores, -1e30)
    maxima = jnp.max(scores, axis=-1, keepdims=True)
    exponent = jnp.exp(scores - maxima)
    weights = (exponent / jnp.sum(exponent, axis=-1, keepdims=True)).astype(jnp.bfloat16)
    attended = jnp.einsum(
        "bhqk,bkhd->bqhd", weights, all_values, preferred_element_type=jnp.float32
    )
    attended = attended.astype(jnp.bfloat16).reshape(-1, part_width)
    partial_value = jnp.dot(attended, w_out, preferred_element_type=jnp.float32)
    tensor_index = lax.axis_index("tensor")
    residual_part = lax.dynamic_slice_in_dim(
        flat_in, tensor_index * part_width, part_width, 1
    ).astype(jnp.float32)
    gain_part = post_gain.astype(jnp.float32)
    summed = lax.psum(partial_value.astype(jnp.bfloat16), "tensor").astype(jnp.float32)
    scale_rows = lax.rsqrt(jnp.mean(summed * summed, axis=-1, keepdims=True) + norm_eps)
    own_share = lax.dynamic_slice_in_dim(summed, tensor_index * part_width, part_width, 1)
    layer_out = (residual_part + own_share * scale_rows * gain_part).astype(jnp.bfloat16)
    return (layer_out.reshape(per_device, span_len, part_width), relaid)


def solution(mesh):
    placed = (
        P("req", None, None),
        P(None, None, "tensor"),
        P(None, "tensor"),
        P("tensor", None),
        P("tensor"),
        P(None, "req", None, "tensor"),
        P(),
        P(),
        P(),
    )
    return jax.shard_map(
        on_device,
        mesh=mesh,
        in_specs=placed,
        out_specs=(P("req", None, "tensor"), P(None, "req", None, "tensor")),
        check_vma=False,
    )
```

profile of v0, /device:TPU:67, one launch (start us, length us, event | category | flops | bytes accessed | tf_op | source)
XLA Modules:
  0.0 268.3 jit_solution(14465095064436898901)
XLA Ops:
  7.2 0.9 reshape.246
  8.4 0.8 copy.79
  9.2 0.6 gather_fusion
  10.3 0.1 broadcast_in_dim.92
  10.5 5.0 %gather_fusion.1 = bf16[64,4,16,512]{3,2,1,0:T(8,128)(2,1)} fusion(bf16[4,64,16,512]{3,2,1,0:T(8,128)(2,1)} %param.14, s32[1024]{0:T(1024)S(1)} %pad_clamp_fusion.1), kind=kCustom, calls=%fused_computation.1 | custom fusion | bytes 8388864 | tf_op jit(solution)/shard_map/jit(_take)/gather | solution.py:46
  15.5 2.6 copy.85
  18.1 0.5 broadcast_select_fusion
  18.6 6.3 %copy.86 = bf16[4,2,1,512,512]{4,1,0,2,3:T(2,128)(2,1)} copy(bf16[4,2,1,512,512]{4,3,1,0,2:T(8,128)(2,1)S(1)} %broadcast_select_fusion) | data formatting | bytes 8388608 | tf_op jit(solution)/shard_map/jit(_take)/select_n | solution.py:46
  24.9 8.9 %all-to-all-start = ((bf16[4,2,1,512,512]{4,1,0,2,3:T(2,128)(2,1)}), bf16[4,2,1,512,512]{4,1,0,2,3:T(2,128)(2,1)}, u32[]{:S(2)}, u32[]{:S(2)}) async-start(bf16[4,2,1,512,512]{4,1,0,2,3:T(2,128)(2,1)} %copy.86), calls=%async_computation | async-start | bytes 8388608 | tf_op jit(solution)/shard_map/all_to_all | solution.py:47
  34.0 0.6 gather_fusion.2
  34.8 10.1 %convolution_bitcast_fusion = f32[3,1024,512]{1,2,0:T(8,128)S(1)} fusion(bf16[3,2048,512]{2,1,0:T(8,128)(2,1)} %param.10, bf16[1024,2048,1]{1,0,2:T(8,128)(2,1)} %bitcast.59), kind=kOutput, calls=%fused_computation.16 | convolution fusion | flops 6442450944 | bytes 16777216 | tf_op jit(solution)/shard_map/rd,mdw->mrw/dot_general | solution.py:60
  44.9 2.6 copy-done.4
  47.6 1.1 slice.84
  48.7 1.8 convert_element_type.42
  50.5 1.1 copy.89
  51.7 5.0 %multiply_reduce_fusion.2 = (f32[1024]{0:T(1024)S(1)}, f32[1024]{0:T(1024)S(1)}, f32[1,1024,512]{1,2,0:T(8,128)}, f32[1,1024,512]{1,2,0:T(8,128)}) fusion(f32[3,1024,512]{1,2,0:T(8,128)} %copy-done.4), kind=kLoop, calls=%fused_computation.31 | loop fusion | flops 2095104 | bytes 8396800 | tf_op jit(solution)/shard_map/reduce_sum | solution.py:65
  56.7 33.9 %all-reduce = (f32[1024]{0:T(1024)S(1)}, f32[1024]{0:T(1024)S(1)}) all-reduce(f32[1024]{0:T(1024)S(1)} %get-tuple-element.18, f32[1024]{0:T(1024)S(1)} %get-tuple-element.17), channel_id=1, replica_groups=mesh['req'=32,'tensor'=4] {'tensor'}, use_global_device_ids=true, to_apply=%region_3.4 | all-reduce | flops 2048 | bytes 16384 | tf_op jit(solution)/shard_map/psum | solution.py:64
  90.7 1.0 multiply_cosine_fusion
  91.7 1.8 multiply_multiply_fusion.1
  93.5 0.2 multiply_multiply_fusion
  93.8 1.9 subtract_convert_fusion.1
  95.7 1.4 concatenate.29
  97.2 1.4 copy.90
  98.5 1.4 concatenate.30
  99.9 1.4 copy.91
  101.3 1.4 concatenate.33
  102.7 1.3 copy.94
  104.1 0.4 concatenate.32
  104.4 1.4 copy.93
  106.0 0.1 broadcast_in_dim.97
  106.1 0.1 broadcast_in_dim.96
  106.2 1.1 pad_add_fusion
  107.3 3.5 %fusion.32 = (bf16[1,2,1,512,512]{4,1,0,2,3:T(2,128)(2,1)S(1)}, bf16[1,2,1,512,512]{4,1,0,2,3:T(2,128)(2,1)}) fusion(bf16[4,2,1,512,512]{4,1,0,2,3:T(2,128)(2,1)} %all-to-all-done), kind=kLoop, calls=%fused_computation.70 | loop fusion | bytes 4194304 | tf_op jit(solution)/shard_map/slice | solution.py:84
  110.8 2.5 copy.87
  113.3 2.4 copy.99
  115.7 1.3 copy.95
  117.0 10.6 %fusion.9 = f32[2,4,512,1024]{3,2,1,0:T(8,128)} fusion(bf16[2,512,4,64]{3,1,2,0:T(8,128)(2,1)} %copy.94, bf16[2,512,4,64]{3,1,2,0:T(8,128)(2,1)} %copy.93, bf16[2,512,4,128]{3,1,2,0:T(8,128)(2,1)} %copy.95, bf16[2,512,4,64]{3,1,2,0:T(8,128)(2,1)} %copy.91, bf16[2,512,4,64]{3,1,2,0:T(8,128)(2,1)} %copy.90), kind=kOutput, calls=%fused_computation.21 | convolution fusion | flops 1082130432 | bytes 19922944 | tf_op jit(solution)/shard_map/bqhd,bkhd->bhqk/dot_general | solution.py:89
  127.7 22.1 %fusion.34 = (f32[2,4,512]{2,1,0:T(4,128)S(1)}, f32[2,4,512,1024]{3,2,1,0:T(8,128)}) fusion(f32[2,4,512,1024]{3,2,1,0:T(8,128)} %fusion.9, pred[2,512,1024]{2,1,0:T(8,128)(4,1)} %pad_add_fusion), kind=kOutput, calls=%fused_computation.72 | output fusion | flops 25166848 | bytes 34619392 | tf_op jit(solution)/shard_map/sub | solution.py:103
  149.7 8.5 %fusion.18 = bf16[2,512,4,128]{1,3,2,0:T(8,128)(2,1)} fusion(f32[2,4,512,1024]{3,2,1,0:T(8,128)} %get-tuple-element.38, f32[2,4,512]{2,1,0:T(4,128)S(1)} %get-tuple-element.37, bf16[2,512,4,128]{1,3,2,0:T(8,128)(2,1)S(1)} %copy-done.5, bf16[2,512,4,128]{1,3,2,0:T(8,128)(2,1)} %bitcast.57), kind=kOutput, calls=%fused_computation.33 | convolution fusion | flops 1086849024 | bytes 19939328 | tf_op jit(solution)/shard_map/bhqk,bkhd->bqhd/dot_general | solution.py:105
  158.2 1.7 copy.96
  160.0 4.3 %convolution_convert_fusion = bf16[1024,2048]{1,0:T(8,128)(2,1)} fusion(bf16[512,2048]{1,0:T(8,128)(2,1)S(1)} %copy-done, bf16[128,8,4,128]{3,2,1,0:T(4,128)(2,1)S(1)} %bitcast.58), kind=kOutput, calls=%fused_computation.15 | convolution fusion | flops 2149580800 | bytes 7340032 | tf_op jit(solution)/shard_map/dot_general | solution.py:109
  164.3 0.6 copy-done.8
  164.9 5.7 %copy.97 = bf16[4,2,512,512]{3,2,1,0:T(8,128)(2,1)} copy(bf16[4,2,512,512]{3,1,0,2:T(2,128)(2,1)} %bitcast.20) | data formatting | bytes 8388608
  170.6 83.7 %all-reduce.3.cloned.1.call-done = bf16[1024,2048]{1,0:T(8,128)(2,1)} async-done(((bf16[1024,2048]{1,0:T(8,128)(2,1)}), bf16[1024,2048]{1,0:T(8,128)(2,1)}) %all-reduce.3.cloned.1.call-update) | async-done | bytes 4194320 | tf_op jit(solution)/shard_map/psum | solution.py:115
  254.4 3.2 %multiply_reduce_fusion = f32[1024]{0:T(1024)S(1)} fusion(bf16[1024,2048]{1,0:T(8,128)(2,1)} %all-reduce.3.cloned.1.call-done), kind=kLoop, calls=%fused_computation.8 | loop fusion | flops 6290432 | bytes 4198400 | tf_op jit(solution)/shard_map/reduce_sum | solution.py:116
  257.6 0.2 copy-done.2
  257.8 1.1 convert_element_type.49
  258.9 2.6 add_convert_fusion
  (46 shorter events, 1.3 us)
Async XLA Ops:
  7.2 152.8 %copy-start = (bf16[512,2048]{1,0:T(8,128)(2,1)S(1)}, bf16[512,2048]{1,0:T(8,128)(2,1)}, u32[]{:S(2)}) copy-start(bf16[512,2048]{1,0:T(8,128)(2,1)} %param.12) | copy-start | bytes 6291460
  24.9 9.0 %copy-start.7 = (s32[64]{0:T(128)S(1)}, s32[64]{0:T(128)}, u32[]{:S(2)}) copy-start(s32[64]{0:T(128)} %param.16) | copy-start | bytes 772
  24.9 9.1 %copy-start.1 = (s32[64]{0:T(128)S(1)}, s32[64]{0:T(128)}, u32[]{:S(2)}) copy-start(s32[64]{0:T(128)} %param.17) | copy-start | bytes 772
  24.9 82.4 %all-to-all-start = ((bf16[4,2,1,512,512]{4,1,0,2,3:T(2,128)(2,1)}), bf16[4,2,1,512,512]{4,1,0,2,3:T(2,128)(2,1)}, u32[]{:S(2)}, u32[]{:S(2)}) async-start(bf16[4,2,1,512,512]{4,1,0,2,3:T(2,128)(2,1)} %copy.86), calls=%async_computation | async-start | bytes 8388608 | tf_op jit(solution)/shard_map/all_to_all | solution.py:47
  33.9 220.5 %all-reduce.3.cloned.1.call-start = ((), (), s32[]{:S(2)}) async-start(), calls=%async_computation.1 | async-start | bytes 8388608 | tf_op jit(solution)/shard_map/psum | solution.py:115
  44.9 2.6 copy-start.4
  51.7 39.0 %copy-start.6 = (bf16[2,512]{1,0:T(2,128)(2,1)S(1)}, bf16[2,512]{1,0:T(2,128)(2,1)}, u32[]{:S(2)}) copy-start(bf16[2,512]{1,0:T(2,128)(2,1)} %param.11) | copy-start | bytes 6148
  90.6 2.9 %copy-start.3 = (f32[1,1024,512]{1,2,0:T(8,128)S(1)}, f32[1,1024,512]{1,2,0:T(8,128)}, u32[]{:S(2)}) copy-start(f32[1,1024,512]{1,2,0:T(8,128)} %get-tuple-element.24) | copy-start | bytes 6291460
  127.7 22.1 %copy-start.5 = (bf16[2,512,4,128]{1,3,2,0:T(8,128)(2,1)S(1)}, bf16[2,512,4,128]{1,3,2,0:T(8,128)(2,1)}, u32[]{:S(2)}) copy-start(bf16[2,512,4,128]{1,3,2,0:T(8,128)(2,1)} %copy.89) | copy-start | bytes 3145732
  164.3 0.7 copy-start.8
  254.4 3.4 %copy-start.2 = (bf16[1024,2048]{1,0:T(8,128)(2,1)S(1)}, bf16[1024,2048]{1,0:T(8,128)(2,1)}, u32[]{:S(2)}) copy-start(bf16[1024,2048]{1,0:T(8,128)(2,1)} %all-reduce.3.cloned.1.call-done) | copy-start | bytes 12582916
Sparse Core Ops, SparseCore 0:
  164.4 89.8 all-reduce.2
where the time goes:
time: 271 us; the launch traced here: 268 us
  waiting for transfers between devices  83.8 us (31%)
  local copies, waits for them, and re-layouts  52.8 us (19%)
  other arithmetic  41 us (15%)
  blocking collectives  33.9 us (13%)
  matrix products  33.5 us (12%)
  between operations  14.3 us (5%)
  starting transfers between devices  8.99 us (3%)
    psum x1, waiting for transfers between devices, on_device(): lax.psum(partial_value.astype(jnp.bfloat16), 'tensor').astype(jnp.float32)  83.7 us
    psum x1, blocking collectives, on_device(): lax.psum((jnp.sum(queries * queries, axis=-1), jnp.sum(keys_new * keys_ne...  33.9 us
    sub x1, other arithmetic, on_device(): exponent = jnp.exp(scores - maxima)  22.1 us
    unnamed x23, local copies, waits for them, and re-layouts  12.5 us
    dot_general x1, matrix products, on_device(): jnp.einsum('bqhd,bkhd->bhqk', query_rot, all_keys, preferred_element_type...  10.6 us
    dot_general x1, matrix products, on_device(): jnp.einsum('rd,mdw->mrw', flat_in, w_qkv, preferred_element_type=jnp.floa...  10.1 us
    concatenate x8, local copies, waits for them, and re-layouts, rotate(): jnp.concatenate([first_half * cosine - second_half * sine_part, second_ha...  10 us
    all_to_all x1, starting transfers between devices, on_device(): lax.all_to_all(gathered.reshape(kv_pool.shape[0], per_device, blocks_each...  8.94 us
  transfers between devices with their start and end apart: 2, of which 1 were waited for; matrix products, arithmetic and copies ran while one was open for 16% of the time, Pallas kernels for 0%

commit v1 on v0

v1 whole, which is shorter than its diff:
```python
import functools
import math

import jax
import jax.numpy as jnp
from jax import lax
from jax.experimental import pallas as pl
from jax.experimental.pallas import tpu as pltpu
from jax.sharding import PartitionSpec as P

MESH = pl.DeviceIdType.MESH
HD = 128
HALF = HD // 2
NORM_EPS = 1e-06
ROPE_BASE = 500000.0
GRID = (4, 4, 2)
NEG = -1e30


def far_first():
    steps = [
        (dz, dy, dx)
        for dz in range(GRID[0])
        for dy in range(GRID[1])
        for dx in range(GRID[2])
    ][1:]

    def hops(step):
        dz, dy, dx = step
        return min(dz, GRID[0] - dz) + min(dy, GRID[1] - dy) + 2 * dx

    return sorted(steps, key=lambda step: -hops(step))


def lane_fold(values):
    total = values[:, :HD]
    for low in range(HD, values.shape[1], HD):
        total = total + values[:, low : low + HD]
    return total


def rows_to_lanes(values):
    return jnp.sum(jnp.transpose(values), axis=0, keepdims=True)


def lanes_to_rows(row):
    return jnp.transpose(jnp.broadcast_to(row, (HD, HD)))


def kernel(
    table_ref,
    order_ref,
    length_ref,
    gain_ref,
    post_ref,
    x_hbm,
    wqkv_hbm,
    wout_hbm,
    pool_hbm,
    out_hbm,
    relaid_hbm,
    pool_a,
    pool_b,
    send_a,
    send_b,
    cache_v,
    x_v,
    w_v,
    wo_v,
    wp_v,
    qk_f,
    qk_b,
    v_b,
    fold_v,
    cos_v,
    sin_v,
    stat_s,
    stat_r,
    att_v,
    attp_v,
    part_s,
    part_r,
    tot_v,
    fin_s,
    fin_r,
    res_v,
    load_sem,
    store_sem,
    a2a_s,
    a2a_r,
    wp_ss,
    wp_rs,
    stat_ss,
    stat_rs,
    att_ss,
    att_rs,
    part_ss,
    part_rs,
    fin_ss,
    fin_rs,
):
    me = lax.axis_index("req")
    t = lax.axis_index("tensor")
    n_req = lax.axis_size("req")
    chip, core = t // 2, lax.rem(t, 2)
    t1 = chip * 2 + 1 - core
    t2 = (1 - chip) * 2 + core
    t3 = (1 - chip) * 2 + 1 - core
    peers = ((me, t1), (me, t2), (me, t3))
    x_at, y_at, z_at = lax.rem(me, 2), lax.rem(me // 2, 4), me // 8
    steps = far_first()

    def at_step(step):
        dz, dy, dx = step
        return (lax.rem(z_at + dz, 4) * 4 + lax.rem(y_at + dy, 4)) * 2 + lax.rem(
            x_at + dx, 2
        )

    targets = [at_step(step) for step in steps]
    span = x_hbm.shape[0] // 2
    width = x_hbm.shape[1]
    part = v_b.shape[1]
    heads = part // HD
    ctx = cache_v.shape[2]
    blk = pool_hbm.shape[2]
    n_pos = pool_hbm.shape[1]
    half = span // 2

    pool_in = [
        pltpu.make_async_copy(
            pool_hbm.at[pl.ds(2 * g, 2)], (pool_a, pool_b)[g], load_sem.at[g]
        )
        for g in range(2)
    ]
    x_in = [
        pltpu.make_async_copy(
            x_hbm.at[pl.ds(k * span, span)],
            x_v.at[pl.ds(k * span, span)],
            load_sem.at[2 + k],
        )
        for k in range(2)
    ]
    w_in = [
        pltpu.make_async_copy(wqkv_hbm.at[m], w_v.at[m], load_sem.at[4 + m])
        for m in range(3)
    ]
    wo_in = pltpu.make_async_copy(wout_hbm, wo_v, load_sem.at[7])
    barrier = pltpu.get_barrier_semaphore()
    for copy in pool_in:
        copy.start()
    for d in targets:
        pl.semaphore_signal(barrier, inc=1, device_id=(d, t), device_id_type=MESH)
    for peer in peers:
        pl.semaphore_signal(barrier, inc=1, device_id=peer, device_id_type=MESH)
    for copy in (x_in[0], w_in[0], w_in[1], x_in[1], w_in[2], wo_in):
        copy.start()

    sends = (send_a, send_b)

    def gather(g):
        pool_v, send_v = (pool_a, pool_b)[g], sends[g]

        def body(p, carry):
            slot = table_ref[order_ref[p], me]
            for plane in range(2):
                send_v[p // 2, plane, lax.rem(p, 2)] = pool_v[plane, slot]
            return carry

        lax.fori_loop(0, n_pos, body, 0, unroll=4)
        own = pl.ds(pl.multiple_of(me * blk, blk), blk)
        for plane in range(2):
            for k in range(2):
                cache_v[2 * g + plane, k, own, :] = send_v[me, plane, k]

    def handover(g):
        own = pl.ds(pl.multiple_of(me * blk, blk), blk)
        return [
            pltpu.make_async_remote_copy(
                sends[g].at[d],
                cache_v.at[pl.ds(2 * g, 2), :, own, :],
                a2a_s.at[g, i],
                a2a_r.at[g, i],
                device_id=(d, t),
                device_id_type=MESH,
            )
            for i, d in enumerate(targets)
        ]

    pool_in[0].wait()
    gather(0)
    pl.semaphore_wait(barrier, len(targets) + len(peers))
    moves = [handover(0), handover(1)]
    for copy in moves[0]:
        copy.start()
    pool_in[1].wait()
    gather(1)

    x_in[0].wait()
    x_in[1].wait()
    w_in[0].wait()
    w_in[1].wait()
    n_half = part // 2

    def qk_tile(i, carry):
        m, k, h = i // 4, lax.rem(i // 2, 2), lax.rem(i, 2)
        rows = pl.ds(pl.multiple_of(k * span, span), span)
        cols = pl.ds(pl.multiple_of(h * n_half, n_half), n_half)
        tile = jnp.dot(
            x_v[rows, :], w_v[m, :, cols], preferred_element_type=jnp.float32
        )
        qk_f[m, rows, cols] = tile
        fold = lane_fold(tile * tile)

        @pl.when(h == 0)
        def _():
            fold_v[m, rows, :] = fold

        @pl.when(h == 1)
        def _():
            fold_v[m, rows, :] = fold_v[m, rows, :] + fold

        return carry

    lax.fori_loop(0, 8, qk_tile, 0)
    groups = 2 * span // HD
    for m in range(2):
        for b in range(groups):
            stat_s[pl.ds(m * groups + b, 1), :] = rows_to_lanes(
                fold_v[m, pl.ds(b * HD, HD), :]
            )

    wo_in.wait()
    wp_moves = [
        pltpu.make_async_remote_copy(
            wo_v.at[:, pl.ds(pl.multiple_of(col * part, part), part)],
            wp_v.at[j],
            wp_ss.at[j],
            wp_rs.at[j],
            device_id=(me, t1),
            device_id_type=MESH,
        )
        for j, col in enumerate((t1, t3))
    ]
    for copy in wp_moves:
        copy.start()
    w_in[2].wait()

    def v_tile(i, carry):
        k, h = i // 2, lax.rem(i, 2)
        rows = pl.ds(pl.multiple_of(k * span, span), span)
        cols = pl.ds(pl.multiple_of(h * n_half, n_half), n_half)
        v_b[rows, cols] = jnp.dot(
            x_v[rows, :], w_v[2, :, cols], preferred_element_type=jnp.float32
        ).astype(jnp.bfloat16)
        return carry

    lax.fori_loop(0, 4, v_tile, 0)
    stat_moves = [
        pltpu.make_async_remote_copy(
            stat_s,
            stat_r.at[j],
            stat_ss.at[j],
            stat_rs.at[j],
            device_id=peer,
            device_id_type=MESH,
        )
        for j, peer in enumerate(peers)
    ]
    for copy in stat_moves:
        copy.start()
    for copy in moves[1]:
        copy.start()

    lens = [length_ref[order_ref[2 * me + k]] for k in range(2)]
    lane = lax.broadcasted_iota(jnp.int32, (1, HD), 1)
    pair = jnp.where(lane < HALF, lane, lane - HALF).astype(jnp.float32)
    frequency = jnp.exp(pair * (-2.0 / HD * math.log(ROPE_BASE)))
    for k in range(2):

        def angle_tile(b, carry, k=k):
            token = lax.broadcasted_iota(jnp.int32, (HD, 1), 0) + b * HD + lens[k]
            angle = token.astype(jnp.float32) * frequency
            rows = pl.ds(pl.multiple_of(k * span + b * HD, HD), HD)
            cos_v[rows, :] = jnp.cos(angle)
            sine = jnp.sin(angle)
            sin_v[rows, :] = jnp.where(lane < HALF, -sine, sine)
            return carry

        lax.fori_loop(0, span // HD, angle_tile, 0)

    for copy in stat_moves:
        copy.wait_recv()
    square = stat_s[...] + stat_r[0] + stat_r[1] + stat_r[2]
    scale = lax.rsqrt(square / width + NORM_EPS)
    for m in range(2):
        for b in range(groups):
            fold_v[m, pl.ds(b * HD, HD), :] = lanes_to_rows(
                scale[m * groups + b : m * groups + b + 1, :]
            )

    def rope_tile(b, carry):
        rows = pl.ds(pl.multiple_of(b * HD, HD), HD)
        cosine, sine = cos_v[rows, :], sin_v[rows, :]
        for m in range(2):
            by_row = fold_v[m, rows, :]
            for h in range(heads):
                cols = pl.ds(h * HD, HD)
                gain = gain_ref[m : m + 1, h * HD : (h + 1) * HD].astype(jnp.float32)
                value = qk_f[m, rows, cols] * by_row * gain
                turned = value * cosine + pltpu.roll(value, HALF, 1) * sine
                qk_b[m, rows, cols] = turned.astype(jnp.bfloat16)
        return carry

    lax.fori_loop(0, groups, rope_tile, 0)

    for copy in moves[0]:
        copy.wait_recv()
    relaid_out = [
        pltpu.make_async_copy(
            cache_v.at[pl.ds(2 * g, 2)], relaid_hbm.at[pl.ds(2 * g, 2)], store_sem.at[g]
        )
        for g in range(2)
    ]
    relaid_out[0].start()

    token_at = lax.broadcasted_iota(jnp.int32, (1, ctx), 1)
    to_base2 = HD**-0.5 * math.log2(math.e)
    causal = lax.broadcasted_iota(jnp.int32, (half, half), 1) <= (
        lax.broadcasted_iota(jnp.int32, (half, half), 0)
    )
    over_rows = (((1,), (1,)), ((), ()))

    def attend(i):
        k, q_at = i // 2, i % 2
        bias = jnp.where(token_at < lens[k], 0.0, NEG)
        seen = half * (q_at + 1)
        new_rows = pl.ds(k * span, seen)

        def head(h, carry):
            cols = pl.ds(pl.multiple_of(h * HD, HD), HD)
            query = qk_b[0, pl.ds(k * span + q_at * half, half), cols]
            old = (
                lax.dot_general(
                    query,
                    cache_v[0, k, :, cols],
                    over_rows,
                    preferred_element_type=jnp.float32,
                )
                + bias
            )
            new = lax.dot_general(
                query,
                qk_b[1, new_rows, cols],
                over_rows,
                preferred_element_type=jnp.float32,
            )
            last = jnp.where(causal, new[:, seen - half :], NEG)
            pieces = [old] + ([new[:, : seen - half]] if q_at else []) + [last]
            top = functools.reduce(
                jnp.maximum, [jnp.max(s, axis=1, keepdims=True) for s in pieces]
            )
            grown = [jnp.exp2((s - top) * to_base2) for s in pieces]
            norm = sum(jnp.sum(e, axis=1, keepdims=True) for e in grown)
            value = jnp.dot(
                grown[0].astype(jnp.bfloat16),
                cache_v[1, k, :, cols],
                preferred_element_type=jnp.float32,
            )
            for j, e in enumerate(grown[1:]):
                value = value + jnp.dot(
                    e.astype(jnp.bfloat16),
                    v_b[pl.ds(k * span + j * half, half), cols],
                    preferred_element_type=jnp.float32,
                )
            att_v[pl.ds(i * half, half), cols] = (value * (1.0 / norm)).astype(
                jnp.bfloat16
            )
            return carry

        lax.fori_loop(0, heads, head, 0)

    att_moves = [
        pltpu.make_async_remote_copy(
            att_v.at[pl.ds(i * half, half)],
            attp_v.at[pl.ds(i * half, half)],
            att_ss.at[i],
            att_rs.at[i],
            device_id=(me, t1),
            device_id_type=MESH,
        )
        for i in range(4)
    ]
    part_moves = [
        pltpu.make_async_remote_copy(
            part_s.at[pl.ds(i * half, half)],
            part_r.at[pl.ds(i * half, half)],
            part_ss.at[i],
            part_rs.at[i],
            device_id=(me, t2),
            device_id_type=MESH,
        )
        for i in range(4)
    ]

    def project(i):
        rows = pl.ds(i * half, half)

        def columns(j, col):
            cols = pl.ds(pl.multiple_of(col * part, part), part)
            return jnp.dot(
                att_v[rows, :], wo_v[:, cols], preferred_element_type=jnp.float32
            ) + jnp.dot(attp_v[rows, :], wp_v[j], preferred_element_type=jnp.float32)

        part_s[rows, :] = columns(1, t2).astype(jnp.bfloat16)
        tot_v[rows, :] = columns(0, t)

    for i in range(4):
        attend(i)
        if i:
            att_moves[i - 1].wait_recv()
            project(i - 1)
            part_moves[i - 1].start()
        att_moves[i].start()
        if i == 0:
            for copy in wp_moves:
                copy.wait_recv()
    att_moves[3].wait_recv()
    project(3)
    part_moves[3].start()

    for copy in moves[1]:
        copy.wait_recv()
    relaid_out[1].start()

    fin_moves = [
        [
            pltpu.make_async_remote_copy(
                fin_s.at[i],
                fin_r.at[i, j],
                fin_ss.at[i, j],
                fin_rs.at[i, j],
                device_id=peer,
                device_id_type=MESH,
            )
            for j, peer in enumerate(peers)
        ]
        for i in range(4)
    ]
    res_out = [
        pltpu.make_async_copy(
            res_v.at[pl.ds(i * half, half)],
            out_hbm.at[pl.ds(i * half, half)],
            store_sem.at[2 + i],
        )
        for i in range(4)
    ]
    own_cols = pl.ds(pl.multiple_of(t * part, part), part)

    def finish(i):
        for copy in fin_moves[i]:
            copy.wait_recv()
        square = fin_s[i] + fin_r[i, 0] + fin_r[i, 1] + fin_r[i, 2]
        scale = lax.rsqrt(square / width + NORM_EPS)
        post = post_ref[...].astype(jnp.float32)
        for b in range(half // HD):
            rows = pl.ds(i * half + b * HD, HD)
            by_row = lanes_to_rows(scale[b : b + 1, :])
            by_row = jnp.concatenate([by_row] * heads, axis=1)
            normed = tot_v[rows, :] * by_row * post
            res_v[rows, :] = (x_v[rows, own_cols].astype(jnp.float32) + normed).astype(
                jnp.bfloat16
            )
        res_out[i].start()

    for i in range(4):
        part_moves[i].wait_recv()
        fin_s[i] = jnp.zeros_like(fin_s[i])
        for b in range(half // HD):
            rows = pl.ds(i * half + b * HD, HD)
            total = tot_v[rows, :] + part_r[rows, :].astype(jnp.float32)
            tot_v[rows, :] = total
            fin_s[i, b : b + 1, :] = rows_to_lanes(lane_fold(total * total))
        for copy in fin_moves[i]:
            copy.start()
        if i:
            finish(i - 1)
    finish(3)

    for g in range(2):
        for copy in moves[g]:
            copy.wait_send()
    for copy in wp_moves + stat_moves + att_moves + part_moves:
        copy.wait_send()
    for group in fin_moves:
        for copy in group:
            copy.wait_send()
    for copy in relaid_out + res_out:
        copy.wait()


def on_device(
    span_in, w_qkv, qk_gain, w_out, post_gain, kv_pool, block_table, request_order, lengths
):
    per_device, span, width = span_in.shape
    part = w_qkv.shape[2]
    planes, n_pos, blk, _ = kv_pool.shape
    rows = per_device * span
    n_req = lax.axis_size("req")
    ctx = block_table.shape[1] * blk
    bf16, f32 = jnp.bfloat16, jnp.float32
    vmem, dma = pltpu.VMEM, pltpu.SemaphoreType.DMA
    smem = pl.BlockSpec(memory_space=pltpu.SMEM)
    in_vmem = pl.BlockSpec(memory_space=pltpu.VMEM)
    stay = pl.BlockSpec(memory_space=pl.ANY)
    stat_rows = 2 * rows // HD
    out, relaid = pl.pallas_call(
        kernel,
        name="handover_layer",
        out_shape=(
            jax.ShapeDtypeStruct((rows, part), bf16),
            jax.ShapeDtypeStruct((planes, per_device, ctx, part), bf16),
        ),
        in_specs=[smem] * 3 + [in_vmem] * 2 + [stay] * 4,
        out_specs=(stay, stay),
        scratch_shapes=[
            vmem((2, n_pos, blk, part), bf16),
            vmem((2, n_pos, blk, part), bf16),
            vmem((n_req, 2, per_device, blk, part), bf16),
            vmem((n_req, 2, per_device, blk, part), bf16),
            vmem((planes, per_device, ctx, part), bf16),
            vmem((rows, width), bf16),
            vmem((3, width, part), bf16),
            vmem((part, width), bf16),
            vmem((2, part, part), bf16),
            vmem((2, rows, part), f32),
            vmem((2, rows, part), bf16),
            vmem((rows, part), bf16),
            vmem((2, rows, HD), f32),
            vmem((rows, HD), f32),
            vmem((rows, HD), f32),
            vmem((stat_rows, HD), f32),
            vmem((3, stat_rows, HD), f32),
            vmem((rows, part), bf16),
            vmem((rows, part), bf16),
            vmem((rows, part), bf16),
            vmem((rows, part), bf16),
            vmem((rows, part), f32),
            vmem((4, 8, HD), f32),
            vmem((4, 3, 8, HD), f32),
            vmem((rows, part), bf16),
            dma((8,)),
            dma((6,)),
            dma((2, n_req)),
            dma((2, n_req)),
            dma((2,)),
            dma((2,)),
            dma((3,)),
            dma((3,)),
            dma((4,)),
            dma((4,)),
            dma((4,)),
            dma((4,)),
            dma((4, 3)),
            dma((4, 3)),
        ],
        compiler_params=pltpu.CompilerParams(
            collective_id=0, has_side_effects=True, vmem_limit_bytes=62 << 20
        ),
    )(
        block_table,
        request_order,
        lengths,
        qk_gain,
        post_gain.reshape(1, part),
        span_in.reshape(rows, width),
        w_qkv,
        w_out,
        kv_pool,
    )
    return out.reshape(per_device, span, part), relaid


def solution(mesh):
    placed = (
        P("req", None, None),
        P(None, None, "tensor"),
        P(None, "tensor"),
        P("tensor", None),
        P("tensor"),
        P(None, "req", None, "tensor"),
        P(),
        P(),
        P(),
    )
    return jax.shard_map(
        on_device,
        mesh=mesh,
        in_specs=placed,
        out_specs=(P("req", None, "tensor"), P(None, "req", None, "tensor")),
        check_vma=False,
    )
```

time: 271 us -> 98.9 us (0.36)
  Pallas kernels: 0 us -> 88.5 us
  waiting for transfers between devices: 83.8 us -> 0 us
  local copies, waits for them, and re-layouts: 52.8 us -> 9.41 us
  other arithmetic: 41 us -> 0 us
  blocking collectives: 33.9 us -> 0 us
  matrix products: 33.5 us -> 0 us
  between operations: 14.3 us -> 0.64 us
  starting transfers between devices: 8.99 us -> 0 us
    pallas_call x0 -> x1, Pallas kernels: none -> 88.5 us  [on_device(): pl.pallas_call(kernel, name='handover_layer', out_shape=(jax.ShapeDtypeSt...]
    psum x1 -> x0, waiting for transfers between devices: 83.7 us -> none  [on_device(): lax.psum(partial_value.astype(jnp.bfloat16), 'tensor').astype(jnp.float32)]
    psum x1 -> x0, blocking collectives: 33.9 us -> none  [on_device(): lax.psum((jnp.sum(queries * queries, axis=-1), jnp.sum(keys_new * keys_ne...]
    dot_general x4 -> x0, matrix products: 33.5 us -> none  [the longest x1 10.6 us: on_device(): jnp.einsum('bqhd,bkhd->bhqk', query_rot, all_keys, preferred_element_type...]
    sub x1 -> x0, other arithmetic: 22.1 us -> none  [on_device(): exponent = jnp.exp(scores - maxima)]
    concatenate x8 -> x0, local copies, waits for them, and re-layouts: 10 us -> none  [rotate(): jnp.concatenate([first_half * cosine - second_half * sine_part, second_ha...]
    all_to_all x1 -> x0, starting transfers between devices: 8.94 us -> none  [on_device(): lax.all_to_all(gathered.reshape(kv_pool.shape[0], per_device, blocks_each...]
    gather x4 -> x0, local copies, waits for them, and re-layouts: 8.89 us -> none  [the longest x2 7.65 us: on_device(): gathered = jnp.take(kv_pool, picked, axis=1)]
  transfers between devices with their start and end apart: 2 -> 0, of which waited for: 1 -> 0; matrix products, arithmetic and copies ran while one was open for 16% -> 0% of each run, Pallas kernels for 0% -> 0%
where the time goes in v1:
time: 98.9 us; the launch traced here: 98.6 us
  Pallas kernels  88.5 us (89%)
  local copies, waits for them, and re-layouts  9.41 us (10%)
    pallas_call x1, Pallas kernels, on_device(): pl.pallas_call(kernel, name='handover_layer', out_shape=(jax.ShapeDtypeSt...  88.5 us
    unnamed x3, local copies, waits for them, and re-layouts  8.15 us

profile of v1, /device:TPU:67, one launch (start us, length us, event | category | flops | bytes accessed | tf_op | source)
XLA Modules:
  0.0 98.6 jit_solution(4976152727135791689)
XLA Ops:
  0.6 1.3 %reshape.13.post_ref = bf16[1,512]{1,0:T(2,128)(2,1)} reshape(bf16[512]{0:T(512)(128)(2,1)} %param.13) | data formatting | bytes 2048 | tf_op jit(solution)/shard_map/reshape | solution.py:574
  1.9 1.4 %copy.11.table_ref = s32[64,32]{1,0:T(8,128)} copy(s32[64,32]{0,1:T(8,128)} %param.15) | data formatting | bytes 16384 | tf_op args[6]
  3.3 88.5 %handover_layer.1 = (bf16[1024,512]{1,0:T(8,128)(2,1)}, bf16[4,2,512,512]{3,2,1,0:T(8,128)(2,1)}) custom-call(s32[64,32]{1,0:T(8,128)} %copy.11.table_ref, s32[64]{0:T(128)} %order_ref.1, s32[64]{0:T(128)} %length_ref.1, bf16[2,512]{1,0:T(2,128)(2,1)} %gain_ref.1, bf16[1,512]{1,0:T(2,128)(2,1)} %reshape.13.post_ref, bf16[1024,2048]{1,0:T(8,128)(2,1)} %bitcast.2, ...), custom_call_target="tpu_custom_call" | custom-call | tf_op jit(solution)/shard_map/handover_layer/pallas_call | solution.py:516
  91.8 2.3 %copy.14 = bf16[2,512,512]{2,1,0:T(8,128)(2,1)} copy(bf16[2,512,512]{2,1,0:T(8,128)(2,1)} %bitcast.3) | data formatting | bytes 2097152
  94.1 4.5 %copy.15 = bf16[4,2,512,512]{3,2,1,0:T(8,128)(2,1)} copy(bf16[4,2,512,512]{3,2,1,0:T(8,128)(2,1)} %get-tuple-element.9) | data formatting | bytes 8388608

commit v2 on v1

--- a/solution.py
+++ b/solution.py
@@ -57,13 +57,12 @@
     wqkv_hbm,
     wout_hbm,
     pool_hbm,
-    out_hbm,
-    relaid_hbm,
+    res_v,
+    cache_v,
     pool_a,
     pool_b,
     send_a,
     send_b,
-    cache_v,
     x_v,
     w_v,
     wo_v,
@@ -83,9 +82,7 @@
     tot_v,
     fin_s,
     fin_r,
-    res_v,
     load_sem,
-    store_sem,
     a2a_s,
     a2a_r,
     wp_ss,
@@ -161,7 +158,7 @@
         pool_v, send_v = (pool_a, pool_b)[g], sends[g]
 
         def body(p, carry):
-            slot = table_ref[order_ref[p], me]
+            slot = table_ref[me, order_ref[p]]
             for plane in range(2):
                 send_v[p // 2, plane, lax.rem(p, 2)] = pool_v[plane, slot]
             return carry
@@ -315,14 +312,6 @@
 
     for copy in moves[0]:
         copy.wait_recv()
-    relaid_out = [
-        pltpu.make_async_copy(
-            cache_v.at[pl.ds(2 * g, 2)], relaid_hbm.at[pl.ds(2 * g, 2)], store_sem.at[g]
-        )
-        for g in range(2)
-    ]
-    relaid_out[0].start()
-
     token_at = lax.broadcasted_iota(jnp.int32, (1, ctx), 1)
     to_base2 = HD**-0.5 * math.log2(math.e)
     causal = lax.broadcasted_iota(jnp.int32, (half, half), 1) <= (
@@ -427,11 +416,6 @@
     att_moves[3].wait_recv()
     project(3)
     part_moves[3].start()
-
-    for copy in moves[1]:
-        copy.wait_recv()
-    relaid_out[1].start()
-
     fin_moves = [
         [
             pltpu.make_async_remote_copy(
@@ -446,14 +430,6 @@
         ]
         for i in range(4)
     ]
-    res_out = [
-        pltpu.make_async_copy(
-            res_v.at[pl.ds(i * half, half)],
-            out_hbm.at[pl.ds(i * half, half)],
-            store_sem.at[2 + i],
-        )
-        for i in range(4)
-    ]
     own_cols = pl.ds(pl.multiple_of(t * part, part), part)
 
     def finish(i):
@@ -461,7 +437,7 @@
             copy.wait_recv()
         square = fin_s[i] + fin_r[i, 0] + fin_r[i, 1] + fin_r[i, 2]
         scale = lax.rsqrt(square / width + NORM_EPS)
-        post = post_ref[...].astype(jnp.float32)
+        post = post_ref[...].astype(jnp.float32)[None, :]
         for b in range(half // HD):
             rows = pl.ds(i * half + b * HD, HD)
             by_row = lanes_to_rows(scale[b : b + 1, :])
@@ -470,7 +446,6 @@
             res_v[rows, :] = (x_v[rows, own_cols].astype(jnp.float32) + normed).astype(
                 jnp.bfloat16
             )
-        res_out[i].start()
 
     for i in range(4):
         part_moves[i].wait_recv()
@@ -486,6 +461,9 @@
             finish(i - 1)
     finish(3)
 
+    for copy in moves[1]:
+        copy.wait_recv()
+
     for g in range(2):
         for copy in moves[g]:
             copy.wait_send()
@@ -494,7 +472,16 @@
     for group in fin_moves:
         for copy in group:
             copy.wait_send()
-    for copy in relaid_out + res_out:
+
+
+def store(res_v, cache_v, out_hbm, relaid_hbm, sem):
+    copies = [pltpu.make_async_copy(res_v, out_hbm, sem.at[0])] + [
+        pltpu.make_async_copy(cache_v.at[plane], relaid_hbm.at[plane], sem.at[1 + plane])
+        for plane in range(cache_v.shape[0])
+    ]
+    for copy in copies:
+        copy.start()
+    for copy in copies:
         copy.wait()
 
 
@@ -517,17 +504,16 @@
         kernel,
         name="handover_layer",
         out_shape=(
-            jax.ShapeDtypeStruct((rows, part), bf16),
-            jax.ShapeDtypeStruct((planes, per_device, ctx, part), bf16),
+            vmem((rows, part), bf16),
+            vmem((planes, per_device, ctx, part), bf16),
         ),
         in_specs=[smem] * 3 + [in_vmem] * 2 + [stay] * 4,
-        out_specs=(stay, stay),
+        out_specs=(in_vmem, in_vmem),
         scratch_shapes=[
             vmem((2, n_pos, blk, part), bf16),
             vmem((2, n_pos, blk, part), bf16),
             vmem((n_req, 2, per_device, blk, part), bf16),
             vmem((n_req, 2, per_device, blk, part), bf16),
-            vmem((planes, per_device, ctx, part), bf16),
             vmem((rows, width), bf16),
             vmem((3, width, part), bf16),
             vmem((part, width), bf16),
@@ -547,9 +533,7 @@
             vmem((rows, part), f32),
             vmem((4, 8, HD), f32),
             vmem((4, 3, 8, HD), f32),
-            vmem((rows, part), bf16),
             dma((8,)),
-            dma((6,)),
             dma((2, n_req)),
             dma((2, n_req)),
             dma((2,)),
@@ -564,19 +548,34 @@
             dma((4, 3)),
         ],
         compiler_params=pltpu.CompilerParams(
-            collective_id=0, has_side_effects=True, vmem_limit_bytes=62 << 20
+            collective_id=0, has_side_effects=True, vmem_limit_bytes=48 << 20
         ),
     )(
-        block_table,
+        block_table.T,
         request_order,
         lengths,
         qk_gain,
-        post_gain.reshape(1, part),
+        post_gain,
         span_in.reshape(rows, width),
         w_qkv,
         w_out,
         kv_pool,
     )
+    out, relaid = (
+        pltpu.with_memory_space_constraint(value, pltpu.VMEM) for value in (out, relaid)
+    )
+    out, relaid = pl.pallas_call(
+        store,
+        name="store_outputs",
+        out_shape=(
+            jax.ShapeDtypeStruct((rows, part), bf16),
+            jax.ShapeDtypeStruct((planes, per_device, ctx, part), bf16),
+        ),
+        in_specs=[in_vmem] * 2,
+        out_specs=(stay, stay),
+        scratch_shapes=[dma((1 + planes,))],
+        compiler_params=pltpu.CompilerParams(vmem_limit_bytes=1 << 20),
+    )(out, relaid)
     return out.reshape(per_device, span, part), relaid
 
 

time: 98.9 us -> 94.2 us (0.952)
  local copies, waits for them, and re-layouts: 9.41 us -> 3.38 us
  Pallas kernels: 88.5 us -> 89.9 us
    unnamed x3 -> x10, local copies, waits for them, and re-layouts: 8.15 us -> 3.38 us
    pallas_call x1 -> x2, Pallas kernels: 88.5 us -> 89.9 us  [the longest x1 87.5 us: on_device(): pl.pallas_call(kernel, name='handover_layer', out_shape=(vmem((rows, part...]
    reshape x1 -> x0, local copies, waits for them, and re-layouts: 1.26 us -> none  [on_device(): post_gain.reshape(1, part)]
where the time goes in v2:
time: 94.2 us; the launch traced here: 94 us
  Pallas kernels  89.9 us (95%)
  local copies, waits for them, and re-layouts  3.38 us (4%)
    pallas_call x1, Pallas kernels, on_device(): pl.pallas_call(kernel, name='handover_layer', out_shape=(vmem((rows, part...  87.5 us
    unnamed x10, local copies, waits for them, and re-layouts  3.38 us
    pallas_call x1, Pallas kernels, on_device(): pl.pallas_call(store, name='store_outputs', out_shape=(jax.ShapeDtypeStru...  2.4 us

profile of v2, /device:TPU:67, one launch (start us, length us, event | category | flops | bytes accessed | tf_op | source)
XLA Modules:
  0.0 94.0 jit_solution(316037502679621951)
XLA Ops:
  0.6 0.0 copy-start
  0.6 0.7 copy-done
  1.4 0.0 copy-start.1
  1.4 0.7 copy-done.1
  2.0 0.0 copy-start.2
  2.0 0.7 copy-done.2
  2.7 0.0 copy-start.3
  2.7 0.7 copy-done.3
  3.4 0.0 copy-start.4
  3.4 0.7 copy-done.4
  4.0 87.5 %handover_layer.1 = (bf16[1024,512]{1,0:T(8,128)(2,1)S(1)}, bf16[4,2,512,512]{3,2,1,0:T(8,128)(2,1)S(1)}) custom-call(s32[32,64]{1,0:T(8,128)S(1)} %bitcast.3, s32[64]{0:T(128)S(1)} %copy-done.3, s32[64]{0:T(128)S(1)} %copy-done.4, bf16[2,512]{1,0:T(2,128)(2,1)S(1)} %copy-done.1, bf16[512]{0:T(512)(128)(2,1)S(1)} %copy-done.2, bf16[1024,2048]{1,0:T(8,128)(2,1)} %bitcast.4, ...), custom_call_target="tpu_custom_call" | custom-call | tf_op jit(solution)/shard_map/handover_layer/pallas_call | solution.py:503
  91.6 2.4 %store_outputs.1 = (bf16[1024,512]{1,0:T(8,128)(2,1)}, bf16[4,2,512,512]{3,2,1,0:T(8,128)(2,1)}) custom-call(bf16[1024,512]{1,0:T(8,128)(2,1)S(1)} %get-tuple-element.6.res_v, bf16[4,2,512,512]{3,2,1,0:T(8,128)(2,1)S(1)} %get-tuple-element.7.cache_v), custom_call_target="tpu_custom_call" | custom-call | tf_op jit(solution)/shard_map/store_outputs/pallas_call | solution.py:567
Async XLA Ops:
  0.6 0.7 copy-start
  1.4 0.7 copy-start.1
  2.0 0.7 copy-start.2
  2.7 0.7 copy-start.3
  3.4 0.7 copy-start.4

commit v3 on v2

--- a/solution.py
+++ b/solution.py
@@ -169,14 +169,14 @@
             for k in range(2):
                 cache_v[2 * g + plane, k, own, :] = send_v[me, plane, k]
 
-    def handover(g):
+    def handover(n, g, low, count):
         own = pl.ds(pl.multiple_of(me * blk, blk), blk)
         return [
             pltpu.make_async_remote_copy(
-                sends[g].at[d],
-                cache_v.at[pl.ds(2 * g, 2), :, own, :],
-                a2a_s.at[g, i],
-                a2a_r.at[g, i],
+                sends[g].at[d, :, pl.ds(low, count)],
+                cache_v.at[pl.ds(2 * g, 2), pl.ds(low, count), own, :],
+                a2a_s.at[n, i],
+                a2a_r.at[n, i],
                 device_id=(d, t),
                 device_id_type=MESH,
             )
@@ -186,8 +186,8 @@
     pool_in[0].wait()
     gather(0)
     pl.semaphore_wait(barrier, len(targets) + len(peers))
-    moves = [handover(0), handover(1)]
-    for copy in moves[0]:
+    moves = [handover(0, 0, 0, 1), handover(1, 0, 1, 1), handover(2, 1, 0, 2)]
+    for copy in moves[0] + moves[1]:
         copy.start()
     pool_in[1].wait()
     gather(1)
@@ -265,7 +265,7 @@
     ]
     for copy in stat_moves:
         copy.start()
-    for copy in moves[1]:
+    for copy in moves[2]:
         copy.start()
 
     lens = [length_ref[order_ref[2 * me + k]] for k in range(2)]
@@ -404,6 +404,9 @@
         tot_v[rows, :] = columns(0, t)
 
     for i in range(4):
+        if i == 2:
+            for copy in moves[1]:
+                copy.wait_recv()
         attend(i)
         if i:
             att_moves[i - 1].wait_recv()
@@ -461,11 +464,11 @@
             finish(i - 1)
     finish(3)
 
-    for copy in moves[1]:
+    for copy in moves[2]:
         copy.wait_recv()
 
-    for g in range(2):
-        for copy in moves[g]:
+    for group in moves:
+        for copy in group:
             copy.wait_send()
     for copy in wp_moves + stat_moves + att_moves + part_moves:
         copy.wait_send()
@@ -534,8 +537,8 @@
             vmem((4, 8, HD), f32),
             vmem((4, 3, 8, HD), f32),
             dma((8,)),
-            dma((2, n_req)),
-            dma((2, n_req)),
+            dma((3, n_req)),
+            dma((3, n_req)),
             dma((2,)),
             dma((2,)),
             dma((3,)),

time: 94.2 us -> 93 us (0.987)
  the two profiles are of different devices: /device:TPU:67 before, /device:TPU:1 now
where the time goes in v3:
time: 93 us; the launch traced here: 92.7 us
  Pallas kernels  88.7 us (95%)
  local copies, waits for them, and re-layouts  3.38 us (4%)
    pallas_call x1, Pallas kernels, on_device(): pl.pallas_call(kernel, name='handover_layer', out_shape=(vmem((rows, part...  86.3 us
    unnamed x10, local copies, waits for them, and re-layouts  3.38 us
    pallas_call x1, Pallas kernels, on_device(): pl.pallas_call(store, name='store_outputs', out_shape=(jax.ShapeDtypeStru...  2.4 us

profile of v3, /device:TPU:1, one launch (start us, length us, event | category | flops | bytes accessed | tf_op | source)
XLA Modules:
  0.0 92.7 jit_solution(7642029937225556862)
XLA Ops:
  0.6 0.0 copy-start
  0.6 0.7 copy-done
  1.4 0.0 copy-start.1
  1.4 0.7 copy-done.1
  2.0 0.0 copy-start.2
  2.0 0.7 copy-done.2
  2.7 0.0 copy-start.3
  2.7 0.7 copy-done.3
  3.4 0.0 copy-start.4
  3.4 0.7 copy-done.4
  4.0 86.3 %handover_layer.1 = (bf16[1024,512]{1,0:T(8,128)(2,1)S(1)}, bf16[4,2,512,512]{3,2,1,0:T(8,128)(2,1)S(1)}) custom-call(s32[32,64]{1,0:T(8,128)S(1)} %bitcast.3, s32[64]{0:T(128)S(1)} %copy-done.3, s32[64]{0:T(128)S(1)} %copy-done.4, bf16[2,512]{1,0:T(2,128)(2,1)S(1)} %copy-done.1, bf16[512]{0:T(512)(128)(2,1)S(1)} %copy-done.2, bf16[1024,2048]{1,0:T(8,128)(2,1)} %bitcast.4, ...), custom_call_target="tpu_custom_call" | custom-call | tf_op jit(solution)/shard_map/handover_layer/pallas_call | solution.py:506
  90.3 2.4 %store_outputs.1 = (bf16[1024,512]{1,0:T(8,128)(2,1)}, bf16[4,2,512,512]{3,2,1,0:T(8,128)(2,1)}) custom-call(bf16[1024,512]{1,0:T(8,128)(2,1)S(1)} %get-tuple-element.6.res_v, bf16[4,2,512,512]{3,2,1,0:T(8,128)(2,1)S(1)} %get-tuple-element.7.cache_v), custom_call_target="tpu_custom_call" | custom-call | tf_op jit(solution)/shard_map/store_outputs/pallas_call | solution.py:570
Async XLA Ops:
  0.6 0.7 copy-start
  1.4 0.7 copy-start.1
  2.0 0.7 copy-start.2
  2.7 0.7 copy-start.3
  3.4 0.7 copy-start.4
